TPU v7x, 128 devices: a whole 4x4x4 slice. The times are simulated.
128 devices in a mesh: row: 16 (over x, z_lo, core), col: 8 (over z_hi, y).
Axes of the slice: x: 4, y: 4, z: 4 (z_hi: 2, z_lo: 2; z = z_hi * 2 + z_lo), core: 2. Of those that a mesh axis runs over, the one named last changes fastest.
Arguments:
- design: float32 [1536, 24576], P(('row', 'col')), may hold values from -6 to 6
- filter_band: float32 [1536, 8], P(('row', 'col')), may hold values from -3 to 3
- arc_lengths: int32 [128, 2], P(('row', 'col')), may hold values from 1 to 11, as said below
Outputs:
- normal: float32 [24576, 24576], P('row', 'col')
Inputs may be any that keep to these rules, and one draw needn't show every extreme that they name: `arc_lengths`: row d gives the lengths of the two arcs held in device d's first slots, in slot order; each row sums to between 2 and 12, some row sums to exactly 12, and all rows together sum to 896.
All inputs are finite; a program needn't handle non-finite values.
Results may differ from a plain program's by a relative error of at most 0.000075.
Values sent between devices are 32-bit elements; how exact they have to be, the bound alone decides.
No kernel may reach another device: no remote copies, remote signals or barrier semaphores. Data moves between devices by JAX's collectives and lax.ppermute only.
A program may use at most 128 MiB of HBM per device.

v0:
```python
import jax
import jax.numpy as jnp
from jax import lax
from jax.sharding import PartitionSpec as P

OBS_DEV = 7


def spread(value, axis, source):
    kept = jnp.where(lax.axis_index(axis) == source, value, 0).astype(value.dtype)
    return lax.psum(kept, axis)


def whiten(design, filter_band, arc_lengths):
    capacity = design.shape[0]
    first_arc = arc_lengths[0, 0]
    filled = first_arc + arc_lengths[0, 1]
    slot_index = jnp.arange(capacity, dtype=jnp.int32)
    position = jnp.where(slot_index < first_arc, slot_index, slot_index - first_arc)
    occupied = slot_index < filled
    whitened = jnp.zeros_like(design)
    for lag_index in range(filter_band.shape[1]):
        shifted = jnp.pad(design, ((lag_index, 0), (0, 0)))[:capacity]
        weight_mask = (occupied & (position >= lag_index)).astype(jnp.float32)[:, None]
        whitened = whitened + filter_band[:, lag_index : lag_index + 1] * weight_mask * shifted
    return whitened


def gram_tile(left_panel, right_panel, live_total):
    product = lax.dot_general(
        left_panel,
        right_panel,
        (((0,), (0,)), ((), ())),
        precision=lax.Precision.HIGHEST,
        preferred_element_type=jnp.float32,
    )
    return product / live_total


def shards(design, filter_band, arc_lengths):
    row_count = lax.axis_size("row")
    col_count = lax.axis_size("col")
    devices = row_count * col_count
    capacity = design.shape[0]
    slab_width = design.shape[1] // devices
    live_total = OBS_DEV * devices
    whitened = whiten(design, filter_band, arc_lengths)
    ordered = (
        whitened.reshape(capacity, col_count, row_count, slab_width)
        .transpose(0, 2, 1, 3)
        .reshape(capacity, devices, slab_width)
    )
    slab_rows = lax.all_to_all(
        ordered, ("row", "col"), split_axis=1, concat_axis=0, tiled=True
    ).reshape(devices * capacity, slab_width)
    right_panel = lax.all_gather(slab_rows, "row", axis=1, tiled=True)
    row_id = lax.axis_index("row")
    root_col = row_id * col_count // row_count
    offset = row_id * col_count % row_count * slab_width
    own_part = lax.dynamic_slice_in_dim(right_panel, offset, col_count * slab_width, 1)
    left_panel = spread(own_part, "col", root_col)
    return gram_tile(left_panel, right_panel, live_total)


def solution(mesh):
    placed = (P(("row", "col"), None), P(("row", "col"), None), P(("row", "col"), None))
    return jax.shard_map(
        shards, mesh=mesh, in_specs=placed, out_specs=P("row", "col"), check_vma=False
    )
```

profile of v0, /device:TPU:96, one launch (start us, length us, event | category | flops | bytes accessed | tf_op | source)
XLA Modules:
  0.0 481.3 jit_solution(18233784695060603784)
XLA Ops:
  6.5 0.0 all-gather.2.cloned.1.call-start
  6.5 1.3 fusion.14
  9.1 1.5 fusion.6
  10.6 6.5 %fusion.3 = f32[12,24576]{1,0:T(8,128)S(1)} fusion(f32[12,24576]{1,0:T(8,128)} %param.3, f32[12]{0:T(128)S(1)} %get-tuple-element.11, f32[12]{0:T(128)S(1)} %get-tuple-element.12, f32[12]{0:T(128)S(1)} %get-tuple-element.6, f32[12]{0:T(128)S(1)} %get-tuple-element.7, f32[12]{0:T(128)S(1)} %get-tuple-element.8, f32[12]{0:T(128)S(1)} %get-tuple-element.9, ...), kind=kLoop, calls=%fused_computation.8 | loop fusion | flops 4423680 | bytes 2359680 | tf_op jit(solution)/shard_map/add | solution.py:25
  17.1 0.7 reshape.90
  17.8 1.1 copy.10
  18.9 0.9 copy.7
  19.9 37.3 %all_to_all.15 = f32[12,128,192]{2,0,1:T(8,128)S(1)} all-to-all(f32[12,128,192]{2,0,1:T(8,128)S(1)} %copy.7), channel_id=1, replica_groups=mesh['row'=16,'col'=8] {'row','col'}, dimensions={1} | all-to-all | bytes 2359296 | tf_op jit(solution)/shard_map/all_to_all | solution.py:53
  57.1 1.3 reshape.92
  58.5 2.9 copy.8
  61.3 0.0 all-gather.2.cloned.1.call-update
  61.4 0.2 all-reduce.9.cloned.1.call-start
  61.6 100.1 %all-gather.2.cloned.1.call-done = f32[1536,3072]{0,1:T(8,128)} async-done(((f32[1536,192]{0,1:T(8,128)}), f32[1536,3072]{0,1:T(8,128)}) %all-gather.2.cloned.1.call-update) | async-done | bytes 18874384 | tf_op jit(solution)/shard_map/all_gather | solution.py:56
  161.7 8.5 %dynamic-slice_select_fusion = f32[1536,1536]{0,1:T(8,128)} fusion(f32[1536,3072]{0,1:T(8,128)} %all-gather.2.cloned.1.call-done, s32[]{:T(128)S(6)} %select_n.65, pred[]{:T(512)S(6)} %eq.5), kind=kLoop, calls=%fused_computation.1 | loop fusion | flops 2359296 | bytes 18874372 | tf_op jit(solution)/shard_map/jit(_where)/select_n | solution.py:10
  170.2 0.0 all-reduce.9.cloned.1.call-update
  170.2 204.8 %all-reduce.9.cloned.1.call-done = f32[1536,1536]{0,1:T(8,128)} async-done(((f32[1536,1536]{0,1:T(8,128)}), f32[1536,1536]{0,1:T(8,128)}) %all-reduce.9.cloned.1.call-update) | async-done | bytes 9437200 | tf_op jit(solution)/shard_map/psum | solution.py:11
  375.0 99.5 %convolution_multiply_fusion = f32[1536,3072]{1,0:T(8,128)} fusion(f32[1536,1536]{0,1:T(8,128)} %all-reduce.9.cloned.1.call-done, f32[1536,3072]{0,1:T(8,128)} %all-gather.2.cloned.1.call-done), kind=kOutput, calls=%fused_computation | convolution fusion | flops 86977806336 | bytes 47185920 | tf_op jit(solution)/shard_map/dot_general | solution.py:30
Async XLA Ops:
  6.5 155.2 %all-gather.2.cloned.1.call-start = ((), (), s32[]{:S(2)}) async-start(), calls=%async_computation.1 | async-start | bytes 20054016 | tf_op jit(solution)/shard_map/all_gather | solution.py:56
  61.4 313.6 %all-reduce.9.cloned.1.call-start = ((), (), s32[]{:S(2)}) async-start(), calls=%async_computation.2 | async-start | bytes 18874368 | tf_op jit(solution)/shard_map/psum | solution.py:11
Sparse Core Ops, SparseCore 0:
  61.5 100.1 all-gather.1
  170.3 204.6 all-reduce.8
where the time goes:
time: 485 us; the launch traced here: 481 us
  waiting for transfers between devices  305 us (63%)
  matrix products  99.5 us (21%)
  blocking collectives  37.3 us (8%)
  other arithmetic  16.5 us (3%)
  between operations  14.7 us (3%)
  local copies, waits for them, and re-layouts  8.26 us (2%)
    psum x1, waiting for transfers between devices, spread(): return lax.psum(kept, axis)  205 us
    all_gather x1, waiting for transfers between devices, shards(): right_panel = lax.all_gather(slab_rows, 'row', axis=1, tiled=True)  100 us
    dot_general x1, matrix products, gram_tile(): lax.dot_general(left_panel, right_panel, (((0,), (0,)), ((), ())), precis...  99.5 us
    all_to_all x1, blocking collectives, shards(): lax.all_to_all(ordered, ('row', 'col'), split_axis=1, concat_axis=0, tile...  37.3 us
  transfers between devices with their start and end apart: 2, of which 2 were waited for; matrix products, arithmetic and copies ran while one was open for 0% of the time, Pallas kernels for 0%

commit v1 on v0

v1 whole, which is shorter than its diff:
```python
import jax
import jax.numpy as jnp
from jax import lax
from jax.experimental import pallas as pl
from jax.experimental.pallas import tpu as pltpu
from jax.sharding import PartitionSpec as P

LIVE = 896
LANES = 128
SLAB = 192
SLOTS = 12
HALF = SLOTS // 2
PIECE = SLOTS + HALF
BLOCK = 2 * PIECE + 1
AXES = ("row", "col")


def whiten_kernel(arcs, taps, design, out):
    first = arcs[0, 0]
    filled = first + arcs[0, 1]
    lag_count = taps.shape[1]
    row = lax.broadcasted_iota(jnp.int32, (SLOTS, lag_count), 0)
    lag = lax.broadcasted_iota(jnp.int32, (SLOTS, lag_count), 1)
    position = jnp.where(row < first, row, row - first)
    weights = jnp.where((row < filled) & (position >= lag), taps[...], 0.0)
    columns = []
    for source in range(SLOTS):
        picked = jnp.where(row - source == lag, weights, 0.0)
        columns.append(jnp.broadcast_to(jnp.sum(picked, axis=1, keepdims=True), (SLOTS, LANES)))
    low_lanes = lax.broadcasted_iota(jnp.int32, (HALF, LANES), 1) < LANES // 2

    def tile(start):
        total = columns[0] * design[pl.ds(0, 1), pl.ds(start, LANES)]
        for source in range(1, SLOTS):
            total = total + columns[source] * design[pl.ds(source, 1), pl.ds(start, LANES)]
        return total

    def pair(index, carry):
        start = index * (3 * LANES)
        left, middle, right = (tile(pl.multiple_of(start + k * LANES, LANES)) for k in range(3))
        upper, lower = middle[:HALF], middle[HALF:]
        even = jnp.where(low_lanes, upper, pltpu.roll(lower, LANES // 2, 1))
        odd = jnp.where(low_lanes, pltpu.roll(upper, LANES // 2, 1), lower)
        for parity, whole, part in ((0, left, even), (1, right, odd)):
            slab = 2 * index + parity
            right_at = ((slab % 16) * 8 + slab // 16) * BLOCK
            left_at = slab * BLOCK + PIECE
            for at in (right_at, left_at):
                out[pl.ds(at, SLOTS), :] = whole
                out[pl.ds(at + SLOTS, HALF), :] = part
        return carry

    lax.fori_loop(0, design.shape[1] // (3 * LANES), pair, 0)
    devices = out.shape[0] // BLOCK
    out[pl.ds(2 * PIECE, devices, stride=BLOCK), :] = jnp.full((devices, LANES), filled, jnp.int32).astype(jnp.float32)


def split(value):
    high = value.astype(jnp.bfloat16)
    return high, (value - high.astype(jnp.float32)).astype(jnp.bfloat16)


def pack_kernel(offsets, received, right_out, left_out, chosen, high, low):
    devices = received.shape[0] // BLOCK
    count = received[pl.ds(2 * PIECE, devices, stride=BLOCK), :]
    later = lax.broadcasted_iota(jnp.int32, (devices, devices), 0) > lax.broadcasted_iota(jnp.int32, (devices, devices), 1)
    start = jnp.dot(later.astype(jnp.bfloat16), count.astype(jnp.bfloat16), preferred_element_type=jnp.float32)
    lane = lax.broadcasted_iota(jnp.int32, (devices, LANES), 1)
    low_lanes = lane < LANES // 2
    lane = lane.astype(jnp.float32)
    for slot in range(SLOTS):
        rows = pl.ds(slot * devices, devices)
        target = jnp.where(count > slot, start + slot, -1.0)
        for group in range(LIVE // LANES):
            chosen[rows, pl.ds(group * LANES, LANES)] = (target - group * LANES == lane).astype(jnp.bfloat16)
        whole = [received[pl.ds(base + slot, devices, stride=BLOCK), :] for base in (0, PIECE)]
        right_part, left_part = (received[pl.ds(base + SLOTS + slot % HALF, devices, stride=BLOCK), :] for base in (0, PIECE))
        if slot < HALF:
            part = jnp.where(low_lanes, right_part, pltpu.roll(left_part, LANES // 2, 1))
        else:
            part = jnp.where(low_lanes, pltpu.roll(right_part, LANES // 2, 1), left_part)
        for index, value in enumerate((*whole, part)):
            high[rows, pl.ds(index * LANES, LANES)], low[rows, pl.ds(index * LANES, LANES)] = split(value)
    contract = (((0,), (0,)), ((), ()))
    packed = lax.dot_general(high[...], chosen[...], contract, preferred_element_type=jnp.float32)
    packed += lax.dot_general(low[...], chosen[...], contract, preferred_element_type=jnp.float32)
    for which, out in enumerate((right_out, left_out)):
        odd = offsets[which]
        out[pl.ds(pl.multiple_of(odd * (LANES // 2), LANES // 2), LANES), :] = packed[which * LANES : (which + 1) * LANES]
        part_at = pl.multiple_of((1 - odd) * LANES, LANES)
        out[pl.ds(part_at, LANES // 2), :] = packed[2 * LANES + which * (LANES // 2) : 2 * LANES + (which + 1) * (LANES // 2)]


def vmem(count):
    return [pl.BlockSpec(memory_space=pltpu.VMEM)] * count


def gram_kernel(left, right, out, turned, left_parts):
    @pl.when(pl.program_id(0) == 0)
    def _():
        high, low = split(left[...])
        left_parts[:, 0:LIVE] = high
        left_parts[:, LIVE : 2 * LIVE] = high
        left_parts[:, 2 * LIVE :] = low

    for group in range(right.shape[0] // LANES):
        rows, lanes = pl.ds(group * LANES, LANES), pl.ds(group * LANES, LANES)
        high, low = split(right[rows, :].T)
        turned[0:LIVE, lanes] = high
        turned[LIVE : 2 * LIVE, lanes] = low
        turned[2 * LIVE :, lanes] = high

    def rows_of(index, carry):
        rows = pl.ds(pl.multiple_of(index * 256, 256), 256)
        out[rows, :] = jnp.dot(left_parts[rows, :], turned[...], preferred_element_type=jnp.float32) * (1.0 / LIVE)
        return carry

    lax.fori_loop(0, left.shape[0] // 256, rows_of, 0)


def whiten(arcs, taps, design):
    return pl.pallas_call(
        whiten_kernel,
        out_shape=jax.ShapeDtypeStruct((128 * BLOCK, LANES), jnp.float32),
        in_specs=[pl.BlockSpec(memory_space=pltpu.SMEM)] + vmem(2),
        out_specs=vmem(1)[0],
        name="whiten",
    )(arcs, taps, design)


def pack(offsets, received):
    slab = jax.ShapeDtypeStruct((SLAB, LIVE), jnp.float32)
    slots = 128 * SLOTS
    return pl.pallas_call(
        pack_kernel,
        out_shape=(slab, slab),
        in_specs=[pl.BlockSpec(memory_space=pltpu.SMEM)] + vmem(1),
        out_specs=tuple(vmem(2)),
        scratch_shapes=[pltpu.VMEM((slots, LIVE), jnp.bfloat16), pltpu.VMEM((slots, 3 * LANES), jnp.bfloat16), pltpu.VMEM((slots, 3 * LANES), jnp.bfloat16)],
        name="pack",
    )(offsets, received)


def gram(left, right):
    rows, columns, width = left.shape[0], right.shape[0], 768
    return pl.pallas_call(
        gram_kernel,
        out_shape=jax.ShapeDtypeStruct((rows, columns), jnp.float32),
        grid=(columns // width,),
        in_specs=[pl.BlockSpec((rows, LIVE), lambda j: (0, 0)), pl.BlockSpec((width, LIVE), lambda j: (j, 0))],
        out_specs=pl.BlockSpec((rows, width), lambda j: (0, j)),
        scratch_shapes=[pltpu.VMEM((3 * LIVE, width), jnp.bfloat16), pltpu.VMEM((rows, 3 * LIVE), jnp.bfloat16)],
        compiler_params=pltpu.CompilerParams(vmem_limit_bytes=60 << 20),
        name="gram",
    )(left, right)


def exchange(value):
    return lax.all_to_all(value.reshape(128, BLOCK, 1, LANES), AXES, split_axis=0, concat_axis=0, tiled=True).reshape(128 * BLOCK, LANES)


def device(row, col):
    return row * 8 + col


def moves(change):
    return [(device(r, c), device(*change(r, c))) for r in range(16) for c in range(8)]


X = {d: moves(lambda r, c, d=d: ((r + 4 * d) % 16, c)) for d in (1, -1)}
Z_LOW = moves(lambda r, c: (r ^ 2, c))
CORE = moves(lambda r, c: (r ^ 1, c))
Y = {d: moves(lambda r, c, d=d: (r, c // 4 * 4 + (c + d) % 4)) for d in (1, -1)}
Z_HIGH = moves(lambda r, c: (r, c ^ 4))


def send(value, pairs):
    return lax.ppermute(value, AXES, pairs)


def ring(own, forward, backward, across):
    before, after = send(own, forward), send(own, backward)
    other = send(own, across)
    other_before, other_after = send(other, forward), send(other, backward)
    far, other_far = send(before, forward), send(other_after, backward)
    return (own, before, far, after), (other, other_before, other_far, other_after)


def assemble_left(slabs, col):
    (own, before, far, after), (other, obefore, ofar, oafter) = slabs
    y = col % 4
    hi = col // 4
    mine = jnp.concatenate([own, before, far, after])
    theirs = jnp.concatenate([other, obefore, ofar, oafter])
    def order(a):
        return jnp.concatenate([lax.dynamic_slice_in_dim(a, ((y - p) % 4) * SLAB, SLAB, 0) for p in range(4)])
    mine, theirs = order(mine), order(theirs)
    return jnp.where(hi == 0, jnp.concatenate([mine, theirs]), jnp.concatenate([theirs, mine]))


def shards(design, taps, arcs):
    row, col = lax.axis_index("row"), lax.axis_index("col")
    offsets = jnp.stack([row % 2, col % 2]).astype(jnp.int32)
    right_slab, left_slab = pack(offsets, exchange(whiten(arcs, taps, design)))
    right_panel = lax.all_gather(right_slab, "row", axis=0, tiled=True)
    left_panel = assemble_left(ring(left_slab, Y[1], Y[-1], Z_HIGH), col)
    return gram(left_panel, right_panel)


def solution(mesh):
    placed = P(AXES, None)
    return jax.shard_map(shards, mesh=mesh, in_specs=(placed, placed, placed), out_specs=P("row", "col"), check_vma=False)
```

time: 485 us -> 193 us (0.40)
  waiting for transfers between devices: 305 us -> 94.4 us
  matrix products: 99.5 us -> 0 us
  Pallas kernels: 0 us -> 55.5 us
  blocking collectives: 37.3 us -> 0 us
  starting transfers between devices: 0.22 us -> 19.5 us
  other arithmetic: 16.5 us -> 3.48 us
    psum x1 -> x0, waiting for transfers between devices: 205 us -> none  [spread(): return lax.psum(kept, axis)]
    all_gather x1, waiting for transfers between devices: 100 us -> 0.01 us  [shards(): right_panel = lax.all_gather(right_slab, 'row', axis=0, tiled=True)]
    dot_general x1 -> x0, matrix products: 99.5 us -> none  [gram_tile(): lax.dot_general(left_panel, right_panel, (((0,), (0,)), ((), ())), precis...]
    ppermute x0 -> x7, waiting for transfers between devices: none -> 63.9 us  [send(): return lax.ppermute(value, AXES, pairs)]
    pallas_call x0 -> x3, Pallas kernels: none -> 55.5 us  [the longest x1 40.6 us: gram(): pl.pallas_call(gram_kernel, out_shape=jax.ShapeDtypeStruct((rows, columns...]
    all_to_all x1 -> x0, blocking collectives: 37.3 us -> none  [shards(): lax.all_to_all(ordered, ('row', 'col'), split_axis=1, concat_axis=0, tile...]
    all_to_all x0 -> x1, waiting for transfers between devices: none -> 30.4 us  [exchange(): lax.all_to_all(value.reshape(128, BLOCK, 1, LANES), AXES, split_axis=0, c...]
    all_to_all x0 -> x1, starting transfers between devices: none -> 9.85 us  [exchange(): lax.all_to_all(value.reshape(128, BLOCK, 1, LANES), AXES, split_axis=0, c...]
  transfers between devices with their start and end apart: 2 -> 9, of which waited for: 2 -> 5; matrix products, arithmetic and copies ran while one was open for 0% -> 4% of each run, Pallas kernels for 0% -> 0%
where the time goes in v1:
time: 193 us
  waiting for transfers between devices  94.4 us (49%)
  Pallas kernels  55.5 us (29%)
  starting transfers between devices  19.5 us (10%)
  between operations  13.6 us (7%)
  local copies, waits for them, and re-layouts  6.21 us (3%)
  other arithmetic  3.48 us (2%)
    ppermute x7, waiting for transfers between devices, send(): return lax.ppermute(value, AXES, pairs)  63.9 us
    pallas_call x1, Pallas kernels, gram(): pl.pallas_call(gram_kernel, out_shape=jax.ShapeDtypeStruct((rows, columns...  40.6 us
    all_to_all x1, waiting for transfers between devices, exchange(): lax.all_to_all(value.reshape(128, BLOCK, 1, LANES), AXES, split_axis=0, c...  30.4 us
    all_to_all x1, starting transfers between devices, exchange(): lax.all_to_all(value.reshape(128, BLOCK, 1, LANES), AXES, split_axis=0, c...  9.85 us
    ppermute x7, starting transfers between devices, send(): return lax.ppermute(value, AXES, pairs)  9.6 us
    pallas_call x1, Pallas kernels, whiten(): pl.pallas_call(whiten_kernel, out_shape=jax.ShapeDtypeStruct((128 * BLOCK...  8.56 us
    pallas_call x1, Pallas kernels, pack(): pl.pallas_call(pack_kernel, out_shape=(slab, slab), in_specs=[pl.BlockSpe...  6.29 us
    unnamed x19, local copies, waits for them, and re-layouts  5.96 us
  transfers between devices with their start and end apart: 9, of which 5 were waited for; matrix products, arithmetic and copies ran while one was open for 4% of the time, Pallas kernels for 0%

profile of v1, /device:TPU:96, one launch (start us, length us, event | category | flops | bytes accessed | tf_op | source)
XLA Modules:
  0.0 192.6 jit_solution(5478236298135961461)
XLA Ops:
  6.5 1.4 copy.6.taps
  7.9 8.6 %whiten.1 = f32[4736,128]{1,0:T(8,128)} custom-call(s32[1,2]{1,0:T(1,128)} %arcs.1, f32[12,8]{1,0:T(8,128)} %copy.6.taps, f32[12,24576]{1,0:T(8,128)} %design.1), custom_call_target="tpu_custom_call" | custom-call | tf_op jit(solution)/shard_map/whiten/pallas_call | solution.py:122
  16.5 9.9 %all-to-all-start = ((f32[128,37,1,128]{3,2,1,0:T(1,128)}), f32[128,37,1,128]{3,2,1,0:T(1,128)S(1)}, u32[]{:S(2)}, u32[]{:S(2)}) async-start(f32[128,37,1,128]{3,2,1,0:T(1,128)} %bitcast.5), calls=%async_computation | async-start | bytes 4849664 | tf_op jit(solution)/shard_map/all_to_all | solution.py:159
  26.4 0.6 pad_add_fusion.offsets
  26.9 30.4 %all-to-all-done = f32[128,37,1,128]{3,2,1,0:T(1,128)S(1)} async-done(((f32[128,37,1,128]{3,2,1,0:T(1,128)}), f32[128,37,1,128]{3,2,1,0:T(1,128)S(1)}, u32[]{:S(2)}, u32[]{:S(2)}) %all-to-all-start) | async-done | bytes 2424864 | tf_op jit(solution)/shard_map/all_to_all | solution.py:159
  57.3 1.4 copy-done
  58.8 6.3 %pack.1 = (f32[192,896]{1,0:T(8,128)}, f32[192,896]{1,0:T(8,128)}) custom-call(s32[2]{0:T(128)} %pad_add_fusion.offsets, f32[4736,128]{1,0:T(8,128)} %bitcast.4), custom_call_target="tpu_custom_call" | custom-call | tf_op jit(solution)/shard_map/pack/pallas_call | solution.py:134
  65.1 2.6 %collective-permute-start.3 = (f32[192,896]{1,0:T(8,128)}, f32[192,896]{1,0:T(8,128)S(1)}, u32[]{:S(2)}, u32[]{:S(2)}) collective-permute-start(f32[192,896]{1,0:T(8,128)} %get-tuple-element.7), channel_id=1, source_target_pairs={{0,4},{1,5},{2,6},{3,7},{4,0},{5,1},{6,2},{7,3},{8,12},{9,13},{10,... | collective-permute-start | bytes 2064392 | tf_op jit(solution)/shard_map/ppermute | solution.py:178
  67.7 0.6 collective-permute-start
  68.2 26.8 %collective-permute-done.3 = f32[192,896]{1,0:T(8,128)S(1)} collective-permute-done((f32[192,896]{1,0:T(8,128)}, f32[192,896]{1,0:T(8,128)S(1)}, u32[]{:S(2)}, u32[]{:S(2)}) %collective-permute-start.3) | collective-permute-done | bytes 688160 | tf_op jit(solution)/shard_map/ppermute | solution.py:178
  95.0 2.0 %collective-permute-start.4 = (f32[192,896]{1,0:T(8,128)S(1)}, f32[192,896]{1,0:T(8,128)S(1)}, u32[]{:S(2)}, u32[]{:S(2)}) collective-permute-start(f32[192,896]{1,0:T(8,128)S(1)} %collective-permute-done.3), channel_id=1, source_target_pairs={{0,1},{1,2},{2,3},{3,0},{4,5},{5,6},{6,7},{7,4},{8,9},{9,10},{10,1... | collective-permute-start | bytes 2064392 | tf_op jit(solution)/shard_map/ppermute | solution.py:178
  97.1 3.2 %collective-permute-start.2 = (f32[192,896]{1,0:T(8,128)}, f32[192,896]{1,0:T(8,128)S(1)}, u32[]{:S(2)}, u32[]{:S(2)}) collective-permute-start(f32[192,896]{1,0:T(8,128)} %get-tuple-element.7), channel_id=1, source_target_pairs={{0,3},{1,0},{2,1},{3,2},{4,7},{5,4},{6,5},{7,6},{8,11},{9,8},{10,9... | collective-permute-start | bytes 2064392 | tf_op jit(solution)/shard_map/ppermute | solution.py:178
  100.3 13.0 %collective-permute-done.5 = f32[192,896]{1,0:T(8,128)S(1)} collective-permute-done((f32[192,896]{1,0:T(8,128)S(1)}, f32[192,896]{1,0:T(8,128)S(1)}, u32[]{:S(2)}, u32[]{:S(2)}) %collective-permute-start.5) | collective-permute-done | bytes 688160 | tf_op jit(solution)/shard_map/ppermute | solution.py:178
  113.3 1.2 collective-permute-start.6
  114.5 1.2 constant_dynamic-update-slice_fusion.3
  115.9 11.9 %collective-permute-done.1 = f32[192,896]{1,0:T(8,128)} collective-permute-done((f32[192,896]{1,0:T(8,128)S(1)}, f32[192,896]{1,0:T(8,128)}, u32[]{:S(2)}, u32[]{:S(2)}) %collective-permute-start.1) | collective-permute-done | bytes 688160 | tf_op jit(solution)/shard_map/ppermute | solution.py:178
  127.8 1.1 constant_dynamic-update-slice_fusion.1
  129.0 12.2 %collective-permute-done.6 = f32[192,896]{1,0:T(8,128)S(1)} collective-permute-done((f32[192,896]{1,0:T(8,128)S(1)}, f32[192,896]{1,0:T(8,128)S(1)}, u32[]{:S(2)}, u32[]{:S(2)}) %collective-permute-start.6) | collective-permute-done | bytes 688160 | tf_op jit(solution)/shard_map/ppermute | solution.py:178
  141.5 0.1 dynamic-slice_dynamic-update-slice_fusion.14
  141.7 0.1 dynamic-slice_dynamic-update-slice_fusion.12
  141.8 0.1 dynamic-slice_dynamic-update-slice_fusion.10
  141.9 0.1 dynamic-slice_dynamic-update-slice_fusion.8
  142.2 2.9 %broadcast_select_fusion.left = f32[1536,896]{1,0:T(8,128)} fusion(f32[1536,896]{1,0:T(8,128)S(1)} %dynamic-slice_dynamic-update-slice_fusion.1, f32[1536,896]{1,0:T(8,128)S(1)} %get-tuple-element.9, pred[]{:T(512)S(6)} %eq.15), kind=kLoop, calls=%fused_computation | loop fusion | flops 1376256 | bytes 16515073 | tf_op jit(solution)/shard_map/jit(_where)/select_n | solution.py:198
  145.2 40.6 %gram.1 = f32[1536,3072]{1,0:T(8,128)} custom-call(f32[1536,896]{1,0:T(8,128)} %broadcast_select_fusion.left, f32[3072,896]{1,0:T(8,128)} %all-gather.2.cloned.1.call-done.right), custom_call_target="tpu_custom_call" | custom-call | tf_op jit(solution)/shard_map/gram/pallas_call | solution.py:146
  (23 shorter events, 0.8 us)
Async XLA Ops:
  16.5 40.9 %all-to-all-start = ((f32[128,37,1,128]{3,2,1,0:T(1,128)}), f32[128,37,1,128]{3,2,1,0:T(1,128)S(1)}, u32[]{:S(2)}, u32[]{:S(2)}) async-start(f32[128,37,1,128]{3,2,1,0:T(1,128)} %bitcast.5), calls=%async_computation | async-start | bytes 4849664 | tf_op jit(solution)/shard_map/all_to_all | solution.py:159
  26.3 118.8 %all-gather.2.cloned.1.call-start = ((), (), s32[]{:S(2)}) async-start(), calls=%async_computation.1 | async-start | bytes 11698176 | tf_op jit(solution)/shard_map/all_gather | solution.py:205
  57.3 1.4 copy-start
  65.1 29.9 %collective-permute-start.3 = (f32[192,896]{1,0:T(8,128)}, f32[192,896]{1,0:T(8,128)S(1)}, u32[]{:S(2)}, u32[]{:S(2)}) collective-permute-start(f32[192,896]{1,0:T(8,128)} %get-tuple-element.7), channel_id=1, source_target_pairs={{0,4},{1,5},{2,6},{3,7},{4,0},{5,1},{6,2},{7,3},{8,12},{9,13},{10,... | collective-permute-start | bytes 2064392 | tf_op jit(solution)/shard_map/ppermute | solution.py:178
  67.7 29.4 %collective-permute-start = (f32[192,896]{1,0:T(8,128)}, f32[192,896]{1,0:T(8,128)S(1)}, u32[]{:S(2)}, u32[]{:S(2)}) collective-permute-start(f32[192,896]{1,0:T(8,128)} %get-tuple-element.7), channel_id=1, source_target_pairs={{0,1},{1,2},{2,3},{3,0},{4,5},{5,6},{6,7},{7,4},{8,9},{9,10},{10,1... | collective-permute-start | bytes 2064392 | tf_op jit(solution)/shard_map/ppermute | solution.py:178
  95.0 18.3 %collective-permute-start.5 = (f32[192,896]{1,0:T(8,128)S(1)}, f32[192,896]{1,0:T(8,128)S(1)}, u32[]{:S(2)}, u32[]{:S(2)}) collective-permute-start(f32[192,896]{1,0:T(8,128)S(1)} %collective-permute-done.3), channel_id=1, source_target_pairs={{0,3},{1,0},{2,1},{3,2},{4,7},{5,4},{6,5},{7,6},{8,11},{9,8},{10,9... | collective-permute-start | bytes 2064392 | tf_op jit(solution)/shard_map/ppermute | solution.py:178
  95.0 20.8 %collective-permute-start.4 = (f32[192,896]{1,0:T(8,128)S(1)}, f32[192,896]{1,0:T(8,128)S(1)}, u32[]{:S(2)}, u32[]{:S(2)}) collective-permute-start(f32[192,896]{1,0:T(8,128)S(1)} %collective-permute-done.3), channel_id=1, source_target_pairs={{0,1},{1,2},{2,3},{3,0},{4,5},{5,6},{6,7},{7,4},{8,9},{9,10},{10,1... | collective-permute-start | bytes 2064392 | tf_op jit(solution)/shard_map/ppermute | solution.py:178
  97.1 30.7 %collective-permute-start.1 = (f32[192,896]{1,0:T(8,128)S(1)}, f32[192,896]{1,0:T(8,128)}, u32[]{:S(2)}, u32[]{:S(2)}) collective-permute-start(f32[192,896]{1,0:T(8,128)S(1)} %collective-permute-done), channel_id=1, source_target_pairs={{0,1},{1,2},{2,3},{3,0},{4,5},{5,6},{6,7},{7,4},{8,9},{9,10},{10,1... | collective-permute-start | bytes 2064392 | tf_op jit(solution)/shard_map/ppermute | solution.py:178
  97.1 31.8 %collective-permute-start.2 = (f32[192,896]{1,0:T(8,128)}, f32[192,896]{1,0:T(8,128)S(1)}, u32[]{:S(2)}, u32[]{:S(2)}) collective-permute-start(f32[192,896]{1,0:T(8,128)} %get-tuple-element.7), channel_id=1, source_target_pairs={{0,3},{1,0},{2,1},{3,2},{4,7},{5,4},{6,5},{7,6},{8,11},{9,8},{10,9... | collective-permute-start | bytes 2064392 | tf_op jit(solution)/shard_map/ppermute | solution.py:178
  113.3 27.9 %collective-permute-start.6 = (f32[192,896]{1,0:T(8,128)S(1)}, f32[192,896]{1,0:T(8,128)S(1)}, u32[]{:S(2)}, u32[]{:S(2)}) collective-permute-start(f32[192,896]{1,0:T(8,128)S(1)} %collective-permute-done.5), channel_id=1, source_target_pairs={{0,3},{1,0},{2,1},{3,2},{4,7},{5,4},{6,5},{7,6},{8,11},{9,8},{10,9... | collective-permute-start | bytes 2064392 | tf_op jit(solution)/shard_map/ppermute | solution.py:178
Sparse Core Ops, SparseCore 0:
  65.2 71.9 all-gather.1

commit v2 on v1

v2 whole, which is shorter than its diff:
```python
import functools

import jax
import jax.numpy as jnp
from jax import lax
from jax.experimental import pallas as pl
from jax.experimental.pallas import tpu as pltpu
from jax.sharding import PartitionSpec as P

LIVE = 896
LANES = 128
SLAB = 192
SLOTS = 12
HALF = SLOTS // 2
PIECE = SLOTS + HALF
BLOCK = 2 * PIECE + 1
AXES = ("row", "col")


def whiten_kernel(arcs, taps, design, out):
    first = arcs[0, 0]
    filled = first + arcs[0, 1]
    lag_count = taps.shape[0]
    lag = lax.broadcasted_iota(jnp.int32, (lag_count, SLOTS), 0)
    slot = lax.broadcasted_iota(jnp.int32, (lag_count, SLOTS), 1)
    position = jnp.where(slot < first, slot, slot - first)
    weights = jnp.where((slot < filled) & (position >= lag), taps[...], 0.0)
    diagonal = lax.broadcasted_iota(jnp.int32, (SLOTS, SLOTS), 0) == lax.broadcasted_iota(jnp.int32, (SLOTS, SLOTS), 1)
    columns = []
    for source in range(SLOTS):
        across = jnp.sum(jnp.where(slot - source == lag, weights, 0.0), axis=0, keepdims=True)
        column = jnp.sum(jnp.where(diagonal, across, 0.0), axis=1, keepdims=True)
        columns.append((jnp.broadcast_to(column[:8], (8, LANES)), jnp.broadcast_to(column[8:], (SLOTS - 8, LANES))))
    low_lanes = lax.broadcasted_iota(jnp.int32, (HALF, LANES), 1) < LANES // 2

    def tile(start):
        rows = [design[pl.ds(source, 1), pl.ds(start, LANES)] for source in range(SLOTS)]
        upper = sum(columns[source][0] * rows[source] for source in range(8))
        lower = sum(columns[source][1] * rows[source] for source in range(9 - lag_count, SLOTS))
        return jnp.concatenate([upper, lower])

    def pair(index, carry):
        start = index * (3 * LANES)
        left, middle, right = (tile(pl.multiple_of(start + k * LANES, LANES)) for k in range(3))
        upper, lower = middle[:HALF], middle[HALF:]
        even = jnp.where(low_lanes, upper, pltpu.roll(lower, LANES // 2, 1))
        odd = jnp.where(low_lanes, pltpu.roll(upper, LANES // 2, 1), lower)
        for parity, whole, part in ((0, left, even), (1, right, odd)):
            slab = 2 * index + parity
            right_at = ((slab % 16) * 8 + slab // 16) * BLOCK
            left_at = slab * BLOCK + PIECE
            for at in (right_at, left_at):
                out[pl.ds(at, SLOTS), :] = whole
                out[pl.ds(at + SLOTS, HALF), :] = part
        return carry

    lax.fori_loop(0, design.shape[1] // (3 * LANES), pair, 0, unroll=4)
    devices = out.shape[0] // BLOCK
    out[pl.ds(2 * PIECE, devices, stride=BLOCK), :] = jnp.full((devices, LANES), filled, jnp.int32).astype(jnp.float32)


def split(value):
    high = value.astype(jnp.bfloat16)
    return high, (value - high.astype(jnp.float32)).astype(jnp.bfloat16)


def pack_kernel(odd, received, right_out, left_out, chosen, high, low):
    devices = received.shape[0] // BLOCK
    count = received[pl.ds(2 * PIECE, devices, stride=BLOCK), :]
    later = lax.broadcasted_iota(jnp.int32, (devices, devices), 0) > lax.broadcasted_iota(jnp.int32, (devices, devices), 1)
    start = jnp.dot(later.astype(jnp.bfloat16), count.astype(jnp.bfloat16), preferred_element_type=jnp.float32)
    count, start = count.T, start.T
    low_lanes = lax.broadcasted_iota(jnp.int32, (devices, LANES), 1) < LANES // 2
    place = lax.broadcasted_iota(jnp.int32, (LANES, devices), 0).astype(jnp.float32)
    for slot in range(SLOTS):
        rows = pl.ds(slot * devices, devices)
        target = jnp.where(count > slot, start + slot, -1.0)
        for group in range(LIVE // LANES):
            chosen[pl.ds(group * LANES, LANES), rows] = (target - group * LANES == place).astype(jnp.bfloat16)
        whole = [received[pl.ds(base + slot, devices, stride=BLOCK), :] for base in (0, PIECE)]
        right_part, left_part = (received[pl.ds(base + SLOTS + slot % HALF, devices, stride=BLOCK), :] for base in (0, PIECE))
        if slot < HALF:
            part = jnp.where(low_lanes, right_part, pltpu.roll(left_part, LANES // 2, 1))
        else:
            part = jnp.where(low_lanes, pltpu.roll(right_part, LANES // 2, 1), left_part)
        for index, value in enumerate((*whole, part)):
            high[rows, pl.ds(index * LANES, LANES)], low[rows, pl.ds(index * LANES, LANES)] = split(value)
    packed = jnp.dot(chosen[...], high[...], preferred_element_type=jnp.float32)
    packed += jnp.dot(chosen[...], low[...], preferred_element_type=jnp.float32)
    part = packed[:, 2 * LANES :]
    right_out[0:LIVE, :] = packed[:, :LANES]
    early, late = part[: LIVE // 2], part[LIVE // 2 :]
    even = jnp.where(jnp.tile(low_lanes[:64], (LIVE // 128, 1)), early, pltpu.roll(late, LANES // 2, 1))
    right_out[LIVE:, :] = jnp.where(odd[0] == 1, pltpu.roll(even, LANES // 2, 1), even)
    left_out[pl.ds(pl.multiple_of(odd[1] * (LANES // 2), LANES // 2), LANES), :] = packed[:, LANES : 2 * LANES].T
    left_out[pl.ds(pl.multiple_of((1 - odd[1]) * LANES, LANES), LANES // 2), :] = part.T[LANES // 2 :]


def vmem(count):
    return [pl.BlockSpec(memory_space=pltpu.VMEM)] * count


WIDE = 4 * SLAB
PAIR = 2 * SLAB
PACKED = LIVE + LIVE // 2
CHUNKS = 4


def chunks_of(first, count):
    return [(first + at, min(2, count - at)) for at in range(0, count, 2)]


def gram_kernel(plan, left_count, fresh_count, ready_count, emitted, sided, where, *refs):
    left_refs, refs = refs[:left_count], refs[left_count:]
    fresh_refs, refs = refs[: 4 * fresh_count], refs[4 * fresh_count :]
    ready_refs, refs = refs[:ready_count], refs[ready_count + sided :]
    out, refs = refs[0], refs[1:]
    emit_refs, refs = refs[:emitted], refs[emitted:]
    left_f, left_parts, right_f, right_parts, stage, left_sem, right_sem, ready_sem, emit_sem, out_sem = refs
    left_copies = [pltpu.make_async_copy(ref, left_f.at[pl.ds(i * SLAB, SLAB)], left_sem.at[i]) for i, ref in enumerate(left_refs)]
    fresh_copies = [pltpu.make_async_copy(ref, right_f.at[i // 4, where[24 + i % 4]], right_sem.at[i]) for i, ref in enumerate(fresh_refs)]
    half = LANES // 2
    low_lanes = lax.broadcasted_iota(jnp.int32, (half, LANES), 1) < half

    def ready_copy(turn):
        index = plan[turn][0] - fresh_count
        return pltpu.make_async_copy(ready_refs[index], right_parts.at[turn % 2], ready_sem.at[index])

    def emit_copy(turn):
        group = plan[turn][0]
        return pltpu.make_async_copy(right_parts.at[turn % 2], emit_refs[group], emit_sem.at[group])

    def is_fresh(turn):
        return plan[turn][0] < fresh_count

    def emits(turn):
        return plan[turn][0] < emitted

    def fetch(turn):
        if is_fresh(turn):
            for copy in fresh_copies[4 * plan[turn][0] : 4 * plan[turn][0] + 4]:
                copy.start()
        elif turn < 2:
            ready_copy(turn).start()

    needed = []
    for _, first, count in plan:
        needed += [index for index in range(first, first + count) if index not in needed]
    fetch(0)
    for index in needed:
        left_copies[index].start()
    for turn in range(1, len(plan)):
        fetch(turn)

    def split_left(index):
        left_copies[index].wait()
        rows = pl.ds(index * SLAB, SLAB)
        high, low = split(left_f[rows, :])
        left_parts[rows, 0:LIVE] = high
        left_parts[rows, LIVE : 2 * LIVE] = high
        left_parts[rows, 2 * LIVE :] = low

    def out_copy(slot, part, side, at, column):
        source = stage.at[slot, pl.ds(part * SLAB, SLAB), pl.ds(side * PAIR, PAIR)]
        return pltpu.make_async_copy(source, out.at[pl.ds(at, SLAB), pl.ds(column, PAIR)], out_sem.at[slot, part, side])

    def wait_stage(turn):
        for index, (_, size) in enumerate(chunks_of(*plan[turn][1:])):
            for part in range(size):
                for side in (0, 1):
                    out_copy((turn % 2) * CHUNKS + index, part, side, 0, 0).wait()

    done = set()
    for turn, (group, first, count) in enumerate(plan):
        buffer = right_parts.at[turn % 2]
        if turn >= 2:
            wait_stage(turn - 2)
        if is_fresh(turn):
            for copy in fresh_copies[4 * group : 4 * group + 4]:
                copy.wait()
            if turn >= 2 and emits(turn - 2):
                emit_copy(turn - 2).wait()

            def split_right(index, carry):
                for side in (0, 1):
                    even, odd = right_f.at[group, 2 * side], right_f.at[group, 2 * side + 1]
                    rows, later = pl.ds(pl.multiple_of(index * half, half), half), pl.ds(pl.multiple_of(LIVE // 2 + index * half, half), half)
                    parts = pl.ds(pl.multiple_of(LIVE + index * half, half), half)
                    one, two = even[parts, :], odd[parts, :]
                    middle = jnp.where(low_lanes, one, two)
                    crossed = pltpu.roll(jnp.where(low_lanes, two, one), half, 1)
                    for tile, (value, after) in enumerate(((even[rows, :], even[later, :]), (middle, crossed), (odd[rows, :], odd[later, :]))):
                        lanes = pl.ds((3 * side + tile) * LANES, LANES)
                        for offset, block in ((0, value), (LIVE // 2, after)):
                            high, low = split(block)
                            for base, piece in ((0, high), (LIVE, low), (2 * LIVE, high)):
                                buffer[pl.ds(pl.multiple_of(base + offset + index * half, half), half), lanes] = piece
                return carry

            lax.fori_loop(0, LIVE // LANES, split_right, 0)
            if emits(turn):
                emit_copy(turn).start()
        else:
            ready_copy(turn).wait()
        if 1 <= turn < len(plan) - 1 and not is_fresh(turn + 1):
            if emits(turn - 1):
                emit_copy(turn - 1).wait()
            ready_copy(turn + 1).start()

        def rows_of(index, begin, size):
            slot = (turn % 2) * CHUNKS + index
            begin = pl.multiple_of(begin * SLAB, SLAB)
            stage[slot, 0 : size * SLAB] = jnp.dot(left_parts[pl.ds(begin, size * SLAB), :], buffer[...], preferred_element_type=jnp.float32) * (1.0 / LIVE)

        def put(index, begin, size):
            for part in range(size):
                at = pl.multiple_of(where[begin + part] * SLAB, SLAB)
                for side in (0, 1):
                    column = pl.multiple_of(where[12 + 2 * group + side] * PAIR, PAIR)
                    out_copy((turn % 2) * CHUNKS + index, part, side, at, column).start()

        chunks = chunks_of(first, count)
        fresh = [index for index in range(first, first + count) if index not in done]
        if turn == 0:
            for index, (begin, size) in enumerate(chunks):
                for at in range(begin, begin + size):
                    split_left(at)
                rows_of(index, begin, size)
                put(index, begin, size)
        else:
            for at in fresh:
                split_left(at)

            def body(index, carry):
                rows_of(index, first + 2 * index, 2)
                put(index, first + 2 * index, 2)
                return carry

            lax.fori_loop(0, count // 2, body, 0)
            if count % 2:
                rows_of(count // 2, *chunks[-1])
                put(count // 2, *chunks[-1])
        done.update(range(first, first + count))
    for turn in range(max(0, len(plan) - 2), len(plan)):
        if emits(turn):
            emit_copy(turn).wait()
        wait_stage(turn)


def gram(plan, lefts, left_at, fresh, ready, right_at, slots, emitted, out):
    fill = jnp.zeros((), jnp.int32)
    where = jnp.stack([*left_at, *[fill] * (12 - len(lefts)), *right_at, *[fill] * (12 - len(right_at)), *slots])
    operands = [*lefts, *[slab for group in fresh for slab in group], *ready]
    blocks = sum(count for _, _, count in plan)
    sided = int(out is not None)
    specs = [pl.BlockSpec(memory_space=pltpu.SMEM)] + [pl.BlockSpec(memory_space=pl.ANY)] * (len(operands) + sided)
    aliases = {len(operands) + 1: 0} if sided else {}
    if sided:
        operands.append(out)
    parts = jax.ShapeDtypeStruct((3 * LIVE, WIDE), jnp.bfloat16)
    return pl.pallas_call(
        functools.partial(gram_kernel, plan, len(lefts), len(fresh), len(ready), emitted, sided),
        out_shape=(jax.ShapeDtypeStruct((1536, 3072), jnp.float32), *[parts] * emitted),
        in_specs=specs,
        out_specs=(pl.BlockSpec(memory_space=pl.ANY),) * (1 + emitted),
        scratch_shapes=[
            pltpu.VMEM((len(lefts) * SLAB, LIVE), jnp.float32),
            pltpu.VMEM((len(lefts) * SLAB, 3 * LIVE), jnp.bfloat16),
            pltpu.VMEM((len(fresh), 4, PACKED, LANES), jnp.float32),
            pltpu.VMEM((2, 3 * LIVE, WIDE), jnp.bfloat16),
            pltpu.VMEM((2 * CHUNKS, PAIR, WIDE), jnp.float32),
            pltpu.SemaphoreType.DMA((len(lefts),)),
            pltpu.SemaphoreType.DMA((4 * len(fresh),)),
            pltpu.SemaphoreType.DMA((max(1, len(ready)),)),
            pltpu.SemaphoreType.DMA((max(1, emitted),)),
            pltpu.SemaphoreType.DMA((2 * CHUNKS, 2, 2)),
        ],
        input_output_aliases=aliases,
        compiler_params=pltpu.CompilerParams(vmem_limit_bytes=52 << 20),
        cost_estimate=pl.CostEstimate(flops=2 * SLAB * WIDE * 3 * LIVE * blocks, bytes_accessed=4 * SLAB * WIDE * blocks, transcendentals=0),
    )(where, *operands)


def whiten(arcs, taps, design):
    return pl.pallas_call(
        whiten_kernel,
        out_shape=jax.ShapeDtypeStruct((128 * BLOCK, LANES), jnp.float32),
        in_specs=[pl.BlockSpec(memory_space=pltpu.SMEM)] + vmem(2),
        out_specs=vmem(1)[0],
        name="whiten",
    )(arcs, taps.T, design)


def pack(odd, received):
    slots = 128 * SLOTS
    return pl.pallas_call(
        pack_kernel,
        out_shape=(jax.ShapeDtypeStruct((PACKED, LANES), jnp.float32), jax.ShapeDtypeStruct((SLAB, LIVE), jnp.float32)),
        in_specs=[pl.BlockSpec(memory_space=pltpu.SMEM)] + vmem(1),
        out_specs=tuple(vmem(2)),
        scratch_shapes=[pltpu.VMEM((LIVE, slots), jnp.bfloat16), pltpu.VMEM((slots, 3 * LANES), jnp.bfloat16), pltpu.VMEM((slots, 3 * LANES), jnp.bfloat16)],
        compiler_params=pltpu.CompilerParams(vmem_limit_bytes=24 << 20),
        name="pack",
    )(odd, received)


def exchange(value):
    return lax.all_to_all(value.reshape(128, BLOCK, 1, LANES), AXES, split_axis=0, concat_axis=0, tiled=True).reshape(128 * BLOCK, LANES)


def device(row, col):
    return row * 8 + col


def moves(change):
    return [(device(r, c), device(*change(r, c))) for r in range(16) for c in range(8)]


X = {d: moves(lambda r, c, d=d: ((r + 4 * d) % 16, c)) for d in (1, -1)}
Z_LOW = moves(lambda r, c: (r ^ 2, c))
CORE = moves(lambda r, c: (r ^ 1, c))
Y = {d: moves(lambda r, c, d=d: (r, c // 4 * 4 + (c + d) % 4)) for d in (1, -1)}
Z_HIGH = moves(lambda r, c: (r, c ^ 4))


def send(value, pairs):
    return lax.ppermute(value, AXES, pairs)


def right_ring(own):
    other = send(own, Z_LOW)
    before, after = send(own, X[1]), send(own, X[-1])
    other_before, other_after = send(other, X[1]), send(other, X[-1])
    far, other_far = send(before, X[1]), send(other_after, X[-1])
    return {(0, 0): own, (0, 1): other, (-1, 0): before, (1, 0): after, (-1, 1): other_before, (1, 1): other_after, (2, 0): far, (2, 1): other_far}


def left_ring(own):
    other = send(own, Z_HIGH)
    before, after = send(own, Y[1]), send(own, Y[-1])
    far = send(before, Y[1])
    other_before, other_after, other_far = send(other, Y[1]), send(other, Y[-1]), send(far, Z_HIGH)
    return {(0, 0): own, (0, 1): other, (-1, 0): before, (1, 0): after, (-1, 1): other_before, (1, 1): other_after, (2, 0): far, (2, 1): other_far}


LEFT_ORDER = ((0, 0), (-1, 0), (1, 0), (0, 1), (2, 0), (-1, 1), (1, 1), (2, 1))
RIGHT_ORDER = ((0, 0), (0, 1), (-1, 0), (1, 0), (-1, 1), (1, 1), (2, 0), (2, 1))


def assemble(design, taps, arcs):
    row, col = lax.axis_index("row"), lax.axis_index("col")
    odd = jnp.stack([row % 2, col % 2]).astype(jnp.int32)
    right, left = pack(odd, exchange(whiten(arcs, taps, design)))
    rights, lefts = right_ring(right), left_ring(left)
    siblings = {key: send(rights[key], CORE) for key in RIGHT_ORDER}
    x, y, high, side, core = row // 4, col % 4, col // 4, row // 2 % 2, row % 2
    groups = [tuple(slab for key in RIGHT_ORDER[i : i + 2] for slab in (rights[key], siblings[key])) for i in range(0, 8, 2)]
    right_at = [(x + step) % 4 * 2 + (side + other) % 2 for step, other in RIGHT_ORDER]
    left_at = [(high + other) % 2 * 4 + (y + step) % 4 for step, other in LEFT_ORDER]
    lefts = [lefts[key] for key in LEFT_ORDER]
    slots = [core, 1 - core, 2 + core, 3 - core]
    out, one, two = gram(((0, 0, 3), (1, 0, 3)), lefts[:3], left_at[:3], groups[:2], [], right_at[:4], slots, 2, None)
    out, three = gram(((1, 3, 2), (2, 3, 2), (0, 0, 5)), lefts[:5], left_at[:5], groups[2:3], [one, two], right_at[4:6] + right_at[:4], slots, 1, out)
    return gram(((1, 5, 3), (2, 5, 3), (3, 5, 3), (0, 0, 8)), lefts, left_at, groups[3:], [one, two, three], right_at[6:] + right_at[:6], slots, 0, out)[0]


def solution(mesh):
    placed = P(AXES, None)
    return jax.shard_map(assemble, mesh=mesh, in_specs=(placed, placed, placed), out_specs=P("row", "col"), check_vma=False)
```

time: 193 us -> 171 us (0.89)
  the two profiles are of different devices: /device:TPU:96 before, /device:TPU:1 now
where the time goes in v2:
time: 171 us
  waiting for transfers between devices  66.4 us (39%)
  Pallas kernels  60.9 us (36%)
  starting transfers between devices  40.4 us (24%)
  local copies, waits for them, and re-layouts  2.85 us (2%)
    pallas_call x3, Pallas kernels, gram(): pl.pallas_call(functools.partial(gram_kernel, plan, len(lefts), len(fresh...  51.6 us
    all_to_all x1, waiting for transfers between devices, exchange(): lax.all_to_all(value.reshape(128, BLOCK, 1, LANES), AXES, split_axis=0, c...  33.5 us
    ppermute x22, waiting for transfers between devices, send(): return lax.ppermute(value, AXES, pairs)  32.9 us
    ppermute x22, starting transfers between devices, send(): return lax.ppermute(value, AXES, pairs)  28.9 us
    all_to_all x1, starting transfers between devices, exchange(): lax.all_to_all(value.reshape(128, BLOCK, 1, LANES), AXES, split_axis=0, c...  11.5 us
    pallas_call x1, Pallas kernels, whiten(): pl.pallas_call(whiten_kernel, out_shape=jax.ShapeDtypeStruct((128 * BLOCK...  4.77 us
    pallas_call x1, Pallas kernels, pack(): pl.pallas_call(pack_kernel, out_shape=(jax.ShapeDtypeStruct((PACKED, LANE...  4.51 us
  transfers between devices with their start and end apart: 23, of which 6 were waited for; matrix products, arithmetic and copies ran while one was open for 0% of the time, Pallas kernels for 17%

profile of v2, /device:TPU:1, one launch (start us, length us, event | category | flops | bytes accessed | tf_op | source)
XLA Modules:
  0.0 171.1 jit_solution(18050450264348308211)
XLA Ops:
  0.0 4.8 %whiten.1 = f32[4736,128]{1,0:T(8,128)} custom-call(s32[1,2]{1,0:T(1,128)} %arcs.1, f32[8,12]{1,0:T(8,128)} %bitcast.26, f32[12,24576]{1,0:T(8,128)} %design.1), custom_call_target="tpu_custom_call" | custom-call | tf_op jit(solution)/shard_map/whiten/pallas_call | solution.py:285
  4.8 11.5 %all-to-all-start = ((f32[128,37,1,128]{3,2,1,0:T(1,128)}), f32[128,37,1,128]{3,2,1,0:T(1,128)S(1)}, u32[]{:S(2)}, u32[]{:S(2)}) async-start(f32[128,37,1,128]{3,2,1,0:T(1,128)} %bitcast.25), calls=%async_computation | async-start | bytes 4849664 | tf_op jit(solution)/shard_map/all_to_all | solution.py:308
  16.4 33.5 %all-to-all-done = f32[128,37,1,128]{3,2,1,0:T(1,128)S(1)} async-done(((f32[128,37,1,128]{3,2,1,0:T(1,128)}), f32[128,37,1,128]{3,2,1,0:T(1,128)S(1)}, u32[]{:S(2)}, u32[]{:S(2)}) %all-to-all-start) | async-done | bytes 2424864 | tf_op jit(solution)/shard_map/all_to_all | solution.py:308
  49.9 4.5 %pack.1 = (f32[1344,128]{1,0:T(8,128)S(1)}, f32[192,896]{1,0:T(8,128)S(1)}) custom-call(s32[2]{0:T(128)S(1)} %pad_add_fusion.odd, f32[4736,128]{1,0:T(8,128)S(1)} %bitcast.24), custom_call_target="tpu_custom_call" | custom-call | tf_op jit(solution)/shard_map/pack/pallas_call | solution.py:296
  55.2 2.0 %collective-permute-start.17 = (f32[1344,128]{1,0:T(8,128)S(1)}, f32[1344,128]{1,0:T(8,128)S(1)}, u32[]{:S(2)}, u32[]{:S(2)}) collective-permute-start(f32[1344,128]{1,0:T(8,128)S(1)} %get-tuple-element.13.refs_3_), channel_id=1, source_target_pairs={{0,96},{1,97},{2,98},{3,99},{4,100},{5,101},{6,102},{7,103},{8,104... | collective-permute-start | bytes 2064392 | tf_op jit(solution)/shard_map/ppermute | solution.py:327
  57.2 0.9 collective-permute-start
  58.1 1.8 %collective-permute-start.1 = (f32[192,896]{1,0:T(8,128)S(1)}, f32[192,896]{1,0:T(8,128)S(1)}, u32[]{:S(2)}, u32[]{:S(2)}) collective-permute-start(f32[192,896]{1,0:T(8,128)S(1)} %get-tuple-element.12.refs_0_), channel_id=1, source_target_pairs={{0,3},{1,0},{2,1},{3,2},{4,7},{5,4},{6,5},{7,6},{8,11},{9,8},{10,9... | collective-permute-start | bytes 2064392 | tf_op jit(solution)/shard_map/ppermute | solution.py:327
  59.9 10.1 %collective-permute-done.10.refs_5_ = f32[1344,128]{1,0:T(8,128)S(1)} collective-permute-done((f32[1344,128]{1,0:T(8,128)S(1)}, f32[1344,128]{1,0:T(8,128)S(1)}, u32[]{:S(2)}, u32[]{:S(2)}) %collective-permute-start.10) | collective-permute-done | bytes 688160 | tf_op jit(solution)/shard_map/ppermute | solution.py:327
  70.0 2.3 %collective-permute-start.14 = (f32[1344,128]{1,0:T(8,128)S(1)}, f32[1344,128]{1,0:T(8,128)S(1)}, u32[]{:S(2)}, u32[]{:S(2)}) collective-permute-start(f32[1344,128]{1,0:T(8,128)S(1)} %get-tuple-element.13.refs_3_), channel_id=1, source_target_pairs={{0,8},{1,9},{2,10},{3,11},{4,12},{5,13},{6,14},{7,15},{8,0},{9,1},... | collective-permute-start | bytes 2064392 | tf_op jit(solution)/shard_map/ppermute | solution.py:327
  72.3 2.8 %collective-permute-start.2 = (f32[192,896]{1,0:T(8,128)S(1)}, f32[192,896]{1,0:T(8,128)S(1)}, u32[]{:S(2)}, u32[]{:S(2)}) collective-permute-start(f32[192,896]{1,0:T(8,128)S(1)} %get-tuple-element.12.refs_0_), channel_id=1, source_target_pairs={{0,4},{1,5},{2,6},{3,7},{4,0},{5,1},{6,2},{7,3},{8,12},{9,13},{10,... | collective-permute-start | bytes 2064392 | tf_op jit(solution)/shard_map/ppermute | solution.py:327
  75.1 1.2 collective-permute-start.15
  76.5 2.7 %collective-permute-start.11 = (f32[1344,128]{1,0:T(8,128)S(1)}, f32[1344,128]{1,0:T(8,128)}, u32[]{:S(2)}, u32[]{:S(2)}) collective-permute-start(f32[1344,128]{1,0:T(8,128)S(1)} %collective-permute-done.10.refs_5_), channel_id=1, source_target_pairs={{0,96},{1,97},{2,98},{3,99},{4,100},{5,101},{6,102},{7,103},{8,104... | collective-permute-start | bytes 2064392 | tf_op jit(solution)/shard_map/ppermute | solution.py:327
  79.1 10.3 %collective-permute-done.2.refs_3_ = f32[192,896]{1,0:T(8,128)S(1)} collective-permute-done((f32[192,896]{1,0:T(8,128)S(1)}, f32[192,896]{1,0:T(8,128)S(1)}, u32[]{:S(2)}, u32[]{:S(2)}) %collective-permute-start.2) | collective-permute-done | bytes 688160 | tf_op jit(solution)/shard_map/ppermute | solution.py:327
  89.4 2.2 %collective-permute-start.18 = (f32[1344,128]{1,0:T(8,128)S(1)}, f32[1344,128]{1,0:T(8,128)S(1)}, u32[]{:S(2)}, u32[]{:S(2)}) collective-permute-start(f32[1344,128]{1,0:T(8,128)S(1)} %collective-permute-done.17.refs_9_), channel_id=1, source_target_pairs={{0,8},{1,9},{2,10},{3,11},{4,12},{5,13},{6,14},{7,15},{8,0},{9,1},... | collective-permute-start | bytes 2064392 | tf_op jit(solution)/shard_map/ppermute | solution.py:327
  92.7 1.6 collective-permute-done.19.refs_5_
  94.3 1.3 collective-permute-start.20
  96.6 2.6 %collective-permute-start.12 = (f32[1344,128]{1,0:T(8,128)}, f32[1344,128]{1,0:T(8,128)}, u32[]{:S(2)}, u32[]{:S(2)}) collective-permute-start(f32[1344,128]{1,0:T(8,128)} %collective-permute-done.11.refs_7_), channel_id=1, source_target_pairs={{0,96},{1,97},{2,98},{3,99},{4,100},{5,101},{6,102},{7,103},{8,104... | collective-permute-start | bytes 2064392 | tf_op jit(solution)/shard_map/ppermute | solution.py:327
  99.5 10.5 %collective-permute-done.3.refs_4_ = f32[192,896]{1,0:T(8,128)} collective-permute-done((f32[192,896]{1,0:T(8,128)S(1)}, f32[192,896]{1,0:T(8,128)}, u32[]{:S(2)}, u32[]{:S(2)}) %collective-permute-start.3) | collective-permute-done | bytes 688160 | tf_op jit(solution)/shard_map/ppermute | solution.py:327
  110.4 2.3 %collective-permute-start.5 = (f32[192,896]{1,0:T(8,128)S(1)}, f32[192,896]{1,0:T(8,128)S(1)}, u32[]{:S(2)}, u32[]{:S(2)}) collective-permute-start(f32[192,896]{1,0:T(8,128)S(1)} %collective-permute-done.2.refs_3_), channel_id=1, source_target_pairs={{0,3},{1,0},{2,1},{3,2},{4,7},{5,4},{6,5},{7,6},{8,11},{9,8},{10,9... | collective-permute-start | bytes 2064392 | tf_op jit(solution)/shard_map/ppermute | solution.py:327
  112.7 2.8 %collective-permute-start.6 = (f32[192,896]{1,0:T(8,128)}, f32[192,896]{1,0:T(8,128)S(1)}, u32[]{:S(2)}, u32[]{:S(2)}) collective-permute-start(f32[192,896]{1,0:T(8,128)} %collective-permute-done.3.refs_4_), channel_id=1, source_target_pairs={{0,4},{1,5},{2,6},{3,7},{4,0},{5,1},{6,2},{7,3},{8,12},{9,13},{10,... | collective-permute-start | bytes 2064392 | tf_op jit(solution)/shard_map/ppermute | solution.py:327
  115.5 1.7 %collective-permute-start.9 = (f32[1344,128]{1,0:T(8,128)}, f32[1344,128]{1,0:T(8,128)S(1)}, u32[]{:S(2)}, u32[]{:S(2)}) collective-permute-start(f32[1344,128]{1,0:T(8,128)} %collective-permute-done.8.refs_8_), channel_id=1, source_target_pairs={{0,8},{1,9},{2,10},{3,11},{4,12},{5,13},{6,14},{7,15},{8,0},{9,1},... | collective-permute-start | bytes 2064392 | tf_op jit(solution)/shard_map/ppermute | solution.py:327
  117.5 13.4 %shard_map.37 = (f32[1536,3072]{1,0:T(8,128)}, bf16[2688,768]{1,0:T(8,128)(2,1)}, bf16[2688,768]{1,0:T(8,128)(2,1)}) custom-call(s32[28]{0:T(128)S(1)} %stack.125.where, f32[192,896]{1,0:T(8,128)S(1)} %get-tuple-element.12.refs_0_, f32[192,896]{1,0:T(8,128)S(1)} %collective-permute-done.refs_1_, f32[192,896]{1,0:T(8,128)} %copy-done.1, f32[1344,128]{1,0:T(8,128)} %copy-done, ...), custom_call_target="tpu_custom_call" | custom-call | flops 4756340736 | bytes 3538944 | tf_op jit(solution)/shard_map/pallas_call | solution.py:261
  131.0 15.1 %shard_map.38 = (f32[1536,3072]{1,0:T(8,128)}, bf16[2688,768]{1,0:T(8,128)(2,1)}) custom-call(s32[28]{0:T(128)S(1)} %stack.126.where, f32[192,896]{1,0:T(8,128)S(1)} %get-tuple-element.12.refs_0_, f32[192,896]{1,0:T(8,128)S(1)} %collective-permute-done.refs_1_, f32[192,896]{1,0:T(8,128)} %copy-done.1, ...), custom_call_target="tpu_custom_call", output_to_operand_aliasing={{0}: (12, {})} | custom-call | flops 7134511104 | bytes 5308416 | tf_op jit(solution)/shard_map/pallas_call | solution.py:261
  147.9 23.1 %shard_map.39 = f32[1536,3072]{1,0:T(8,128)} custom-call(s32[28]{0:T(128)S(1)} %stack.122.where, f32[192,896]{1,0:T(8,128)S(1)} %get-tuple-element.12.refs_0_, f32[192,896]{1,0:T(8,128)S(1)} %collective-permute-done.refs_1_, f32[192,896]{1,0:T(8,128)} %copy-done.1, f32[192,896]{1,0:T(8,128)} %copy-done.2, ...), custom_call_target="tpu_custom_call", output_to_operand_aliasing={{}: (16, {})} | custom-call | flops 13476298752 | bytes 10027008 | tf_op jit(solution)/shard_map/pallas_call | solution.py:261
  (62 shorter events, 5.6 us)
Async XLA Ops:
  4.8 45.1 %all-to-all-start = ((f32[128,37,1,128]{3,2,1,0:T(1,128)}), f32[128,37,1,128]{3,2,1,0:T(1,128)S(1)}, u32[]{:S(2)}, u32[]{:S(2)}) async-start(f32[128,37,1,128]{3,2,1,0:T(1,128)} %bitcast.25), calls=%async_computation | async-start | bytes 4849664 | tf_op jit(solution)/shard_map/all_to_all | solution.py:308
  54.4 15.6 %collective-permute-start.10 = (f32[1344,128]{1,0:T(8,128)S(1)}, f32[1344,128]{1,0:T(8,128)S(1)}, u32[]{:S(2)}, u32[]{:S(2)}) collective-permute-start(f32[1344,128]{1,0:T(8,128)S(1)} %get-tuple-element.13.refs_3_), channel_id=1, source_target_pairs={{0,16},{1,17},{2,18},{3,19},{4,20},{5,21},{6,22},{7,23},{8,24},{9,... | collective-permute-start | bytes 2064392 | tf_op jit(solution)/shard_map/ppermute | solution.py:327
  54.5 17.8 %collective-permute-start.7 = (f32[1344,128]{1,0:T(8,128)S(1)}, f32[1344,128]{1,0:T(8,128)}, u32[]{:S(2)}, u32[]{:S(2)}) collective-permute-start(f32[1344,128]{1,0:T(8,128)S(1)} %get-tuple-element.13.refs_3_), channel_id=1, source_target_pairs={{0,32},{1,33},{2,34},{3,35},{4,36},{5,37},{6,38},{7,39},{8,40},{9,... | collective-permute-start | bytes 2064392 | tf_op jit(solution)/shard_map/ppermute | solution.py:327
  55.2 19.9 %collective-permute-start.17 = (f32[1344,128]{1,0:T(8,128)S(1)}, f32[1344,128]{1,0:T(8,128)S(1)}, u32[]{:S(2)}, u32[]{:S(2)}) collective-permute-start(f32[1344,128]{1,0:T(8,128)S(1)} %get-tuple-element.13.refs_3_), channel_id=1, source_target_pairs={{0,96},{1,97},{2,98},{3,99},{4,100},{5,101},{6,102},{7,103},{8,104... | collective-permute-start | bytes 2064392 | tf_op jit(solution)/shard_map/ppermute | solution.py:327
  57.2 19.1 %collective-permute-start = (f32[192,896]{1,0:T(8,128)S(1)}, f32[192,896]{1,0:T(8,128)S(1)}, u32[]{:S(2)}, u32[]{:S(2)}) collective-permute-start(f32[192,896]{1,0:T(8,128)S(1)} %get-tuple-element.12.refs_0_), channel_id=1, source_target_pairs={{0,1},{1,2},{2,3},{3,0},{4,5},{5,6},{6,7},{7,4},{8,9},{9,10},{10,1... | collective-permute-start | bytes 2064392 | tf_op jit(solution)/shard_map/ppermute | solution.py:327
  58.1 18.4 %collective-permute-start.1 = (f32[192,896]{1,0:T(8,128)S(1)}, f32[192,896]{1,0:T(8,128)S(1)}, u32[]{:S(2)}, u32[]{:S(2)}) collective-permute-start(f32[192,896]{1,0:T(8,128)S(1)} %get-tuple-element.12.refs_0_), channel_id=1, source_target_pairs={{0,3},{1,0},{2,1},{3,2},{4,7},{5,4},{6,5},{7,6},{8,11},{9,8},{10,9... | collective-permute-start | bytes 2064392 | tf_op jit(solution)/shard_map/ppermute | solution.py:327
  70.0 6.5 %collective-permute-start.14 = (f32[1344,128]{1,0:T(8,128)S(1)}, f32[1344,128]{1,0:T(8,128)S(1)}, u32[]{:S(2)}, u32[]{:S(2)}) collective-permute-start(f32[1344,128]{1,0:T(8,128)S(1)} %get-tuple-element.13.refs_3_), channel_id=1, source_target_pairs={{0,8},{1,9},{2,10},{3,11},{4,12},{5,13},{6,14},{7,15},{8,0},{9,1},... | collective-permute-start | bytes 2064392 | tf_op jit(solution)/shard_map/ppermute | solution.py:327
  72.3 17.1 %collective-permute-start.2 = (f32[192,896]{1,0:T(8,128)S(1)}, f32[192,896]{1,0:T(8,128)S(1)}, u32[]{:S(2)}, u32[]{:S(2)}) collective-permute-start(f32[192,896]{1,0:T(8,128)S(1)} %get-tuple-element.12.refs_0_), channel_id=1, source_target_pairs={{0,4},{1,5},{2,6},{3,7},{4,0},{5,1},{6,2},{7,3},{8,12},{9,13},{10,... | collective-permute-start | bytes 2064392 | tf_op jit(solution)/shard_map/ppermute | solution.py:327
  75.1 16.6 %collective-permute-start.15 = (f32[1344,128]{1,0:T(8,128)S(1)}, f32[1344,128]{1,0:T(8,128)S(1)}, u32[]{:S(2)}, u32[]{:S(2)}) collective-permute-start(f32[1344,128]{1,0:T(8,128)S(1)} %collective-permute-done.10.refs_5_), channel_id=1, source_target_pairs={{0,8},{1,9},{2,10},{3,11},{4,12},{5,13},{6,14},{7,15},{8,0},{9,1},... | collective-permute-start | bytes 2064392 | tf_op jit(solution)/shard_map/ppermute | solution.py:327
  76.4 15.8 %collective-permute-start.16 = (f32[1344,128]{1,0:T(8,128)}, f32[1344,128]{1,0:T(8,128)S(1)}, u32[]{:S(2)}, u32[]{:S(2)}) collective-permute-start(f32[1344,128]{1,0:T(8,128)} %collective-permute-done.7.refs_7_), channel_id=1, source_target_pairs={{0,8},{1,9},{2,10},{3,11},{4,12},{5,13},{6,14},{7,15},{8,0},{9,1},... | collective-permute-start | bytes 2064392 | tf_op jit(solution)/shard_map/ppermute | solution.py:327
  76.4 17.9 %collective-permute-start.19 = (f32[1344,128]{1,0:T(8,128)S(1)}, f32[1344,128]{1,0:T(8,128)}, u32[]{:S(2)}, u32[]{:S(2)}) collective-permute-start(f32[1344,128]{1,0:T(8,128)S(1)} %collective-permute-done.10.refs_5_), channel_id=1, source_target_pairs={{0,32},{1,33},{2,34},{3,35},{4,36},{5,37},{6,38},{7,39},{8,40},{9,... | collective-permute-start | bytes 2064392 | tf_op jit(solution)/shard_map/ppermute | solution.py:327
  76.5 19.1 %collective-permute-start.11 = (f32[1344,128]{1,0:T(8,128)S(1)}, f32[1344,128]{1,0:T(8,128)}, u32[]{:S(2)}, u32[]{:S(2)}) collective-permute-start(f32[1344,128]{1,0:T(8,128)S(1)} %collective-permute-done.10.refs_5_), channel_id=1, source_target_pairs={{0,96},{1,97},{2,98},{3,99},{4,100},{5,101},{6,102},{7,103},{8,104... | collective-permute-start | bytes 2064392 | tf_op jit(solution)/shard_map/ppermute | solution.py:327
  89.4 41.6 %copy-start.2 = (f32[192,896]{1,0:T(8,128)}, f32[192,896]{1,0:T(8,128)S(1)}, u32[]{:S(2)}) copy-start(f32[192,896]{1,0:T(8,128)S(1)} %collective-permute-done.2.refs_3_) | copy-start | bytes 2064388
  89.4 6.3 %collective-permute-start.18 = (f32[1344,128]{1,0:T(8,128)S(1)}, f32[1344,128]{1,0:T(8,128)S(1)}, u32[]{:S(2)}, u32[]{:S(2)}) collective-permute-start(f32[1344,128]{1,0:T(8,128)S(1)} %collective-permute-done.17.refs_9_), channel_id=1, source_target_pairs={{0,8},{1,9},{2,10},{3,11},{4,12},{5,13},{6,14},{7,15},{8,0},{9,1},... | collective-permute-start | bytes 2064392 | tf_op jit(solution)/shard_map/ppermute | solution.py:327
  91.7 18.4 %collective-permute-start.3 = (f32[192,896]{1,0:T(8,128)S(1)}, f32[192,896]{1,0:T(8,128)}, u32[]{:S(2)}, u32[]{:S(2)}) collective-permute-start(f32[192,896]{1,0:T(8,128)S(1)} %collective-permute-done.refs_1_), channel_id=1, source_target_pairs={{0,1},{1,2},{2,3},{3,0},{4,5},{5,6},{6,7},{7,4},{8,9},{9,10},{10,1... | collective-permute-start | bytes 2064392 | tf_op jit(solution)/shard_map/ppermute | solution.py:327
  92.2 18.2 %collective-permute-start.8 = (f32[1344,128]{1,0:T(8,128)}, f32[1344,128]{1,0:T(8,128)}, u32[]{:S(2)}, u32[]{:S(2)}) collective-permute-start(f32[1344,128]{1,0:T(8,128)} %collective-permute-done.7.refs_7_), channel_id=1, source_target_pairs={{0,32},{1,33},{2,34},{3,35},{4,36},{5,37},{6,38},{7,39},{8,40},{9,... | collective-permute-start | bytes 2064392 | tf_op jit(solution)/shard_map/ppermute | solution.py:327
  94.3 18.4 %collective-permute-start.20 = (f32[1344,128]{1,0:T(8,128)}, f32[1344,128]{1,0:T(8,128)}, u32[]{:S(2)}, u32[]{:S(2)}) collective-permute-start(f32[1344,128]{1,0:T(8,128)} %collective-permute-done.19.refs_5_), channel_id=1, source_target_pairs={{0,8},{1,9},{2,10},{3,11},{4,12},{5,13},{6,14},{7,15},{8,0},{9,1},... | collective-permute-start | bytes 2064392 | tf_op jit(solution)/shard_map/ppermute | solution.py:327
  95.6 19.9 %collective-permute-start.21 = (f32[1344,128]{1,0:T(8,128)}, f32[1344,128]{1,0:T(8,128)}, u32[]{:S(2)}, u32[]{:S(2)}) collective-permute-start(f32[1344,128]{1,0:T(8,128)} %collective-permute-done.11.refs_7_), channel_id=1, source_target_pairs={{0,8},{1,9},{2,10},{3,11},{4,12},{5,13},{6,14},{7,15},{8,0},{9,1},... | collective-permute-start | bytes 2064392 | tf_op jit(solution)/shard_map/ppermute | solution.py:327
  96.6 20.7 %collective-permute-start.12 = (f32[1344,128]{1,0:T(8,128)}, f32[1344,128]{1,0:T(8,128)}, u32[]{:S(2)}, u32[]{:S(2)}) collective-permute-start(f32[1344,128]{1,0:T(8,128)} %collective-permute-done.11.refs_7_), channel_id=1, source_target_pairs={{0,96},{1,97},{2,98},{3,99},{4,100},{5,101},{6,102},{7,103},{8,104... | collective-permute-start | bytes 2064392 | tf_op jit(solution)/shard_map/ppermute | solution.py:327
  110.1 36.1 %collective-permute-start.4 = (f32[192,896]{1,0:T(8,128)S(1)}, f32[192,896]{1,0:T(8,128)S(1)}, u32[]{:S(2)}, u32[]{:S(2)}) collective-permute-start(f32[192,896]{1,0:T(8,128)S(1)} %collective-permute-done.2.refs_3_), channel_id=1, source_target_pairs={{0,1},{1,2},{2,3},{3,0},{4,5},{5,6},{6,7},{7,4},{8,9},{9,10},{10,1... | collective-permute-start | bytes 2064392 | tf_op jit(solution)/shard_map/ppermute | solution.py:327
  110.4 35.7 %collective-permute-start.5 = (f32[192,896]{1,0:T(8,128)S(1)}, f32[192,896]{1,0:T(8,128)S(1)}, u32[]{:S(2)}, u32[]{:S(2)}) collective-permute-start(f32[192,896]{1,0:T(8,128)S(1)} %collective-permute-done.2.refs_3_), channel_id=1, source_target_pairs={{0,3},{1,0},{2,1},{3,2},{4,7},{5,4},{6,5},{7,6},{8,11},{9,8},{10,9... | collective-permute-start | bytes 2064392 | tf_op jit(solution)/shard_map/ppermute | solution.py:327
  112.7 33.4 %collective-permute-start.6 = (f32[192,896]{1,0:T(8,128)}, f32[192,896]{1,0:T(8,128)S(1)}, u32[]{:S(2)}, u32[]{:S(2)}) collective-permute-start(f32[192,896]{1,0:T(8,128)} %collective-permute-done.3.refs_4_), channel_id=1, source_target_pairs={{0,4},{1,5},{2,6},{3,7},{4,0},{5,1},{6,2},{7,3},{8,12},{9,13},{10,... | collective-permute-start | bytes 2064392 | tf_op jit(solution)/shard_map/ppermute | solution.py:327
  115.5 30.6 %collective-permute-start.9 = (f32[1344,128]{1,0:T(8,128)}, f32[1344,128]{1,0:T(8,128)S(1)}, u32[]{:S(2)}, u32[]{:S(2)}) collective-permute-start(f32[1344,128]{1,0:T(8,128)} %collective-permute-done.8.refs_8_), channel_id=1, source_target_pairs={{0,8},{1,9},{2,10},{3,11},{4,12},{5,13},{6,14},{7,15},{8,0},{9,1},... | collective-permute-start | bytes 2064392 | tf_op jit(solution)/shard_map/ppermute | solution.py:327
  117.3 28.9 %collective-permute-start.13 = (f32[1344,128]{1,0:T(8,128)}, f32[1344,128]{1,0:T(8,128)S(1)}, u32[]{:S(2)}, u32[]{:S(2)}) collective-permute-start(f32[1344,128]{1,0:T(8,128)} %collective-permute-done.12.refs_10_), channel_id=1, source_target_pairs={{0,8},{1,9},{2,10},{3,11},{4,12},{5,13},{6,14},{7,15},{8,0},{9,1},... | collective-permute-start | bytes 2064392 | tf_op jit(solution)/shard_map/ppermute | solution.py:327
  (13 other events, 154.6 us)
